TPU v7x, 256 devices: a whole 4x4x8 slice. The times are simulated.
256 devices in a mesh: scene: 128 (over x_lo, y, z, core), tile: 2 (over x_hi).
Axes of the slice: x: 4 (x_hi: 2, x_lo: 2; x = x_hi * 2 + x_lo), y: 4, z: 8, core: 2. Of those that a mesh axis runs over, the one named last changes fastest.
Arguments:
- features_in: bfloat16 [128, 4, 64, 4096], P('scene', 'tile'), may hold values from -6 to 6
- strided_weights: bfloat16 [2, 64, 1024], replicated, may hold values from -0.1875 to 0.1875
- dilated_weights: bfloat16 [2, 64, 576], replicated, may hold values from -0.25 to 0.25
- tile_bias: float32 [256, 64], replicated, may hold values from -3 to 3
- cost_cotangent: bfloat16 [128, 4, 1024], P('scene', 'tile'), may hold values from -6 to 6
- footprint_pairing: int32 [64, 4], replicated, may hold values from 0 to 3, each once within a row
- valid_counts: int32 [64], replicated, may hold values from 1 to 4, as said below
- tile_owner: int32 [128], replicated, may hold values from 0 to 255, as said below
Outputs:
- grad_features: bfloat16 [128, 4, 64, 4096], P('scene', 'tile')
- grad_weights: float32 [128, 1600], P('scene')
- grad_bias: float32 [256, 64], P(('scene', 'tile'))
Inputs may be any that keep to these rules, and one draw needn't show every extreme that they name: `footprint_pairing`: row k maps each patch of scene 2k to the patch of scene 2k + 1 that covers its footprint; each row is a permutation. `valid_counts`: patches 0 to count - 1 of both scenes of a pair are live; some pair has all 4 live. `tile_owner`: several scenes may share a tile, and many tiles have no scene.
All inputs are finite; a program needn't handle non-finite values.
Results may differ from a plain program's by a relative error of at most 0.007.
Values may be sent and summed in bfloat16 or wider, within the bound.
A program may use at most 64 MiB of HBM per device.

v0:
```python
import math

import jax
import jax.numpy as jnp
from jax import lax
from jax.sharding import PartitionSpec as P


def from_partner(x, axis, distance):
    return lax.ppermute(x, axis, [(i, i ^ 1 << distance) for i in range(lax.axis_size(axis))])


def apply_convolution(
    left_operand,
    right_operand,
    window_strides,
    border_padding,
    left_dilation,
    right_dilation,
    dimension_labels,
):
    return lax.conv_general_dilated(
        left_operand,
        right_operand,
        window_strides,
        border_padding,
        lhs_dilation=left_dilation,
        rhs_dilation=right_dilation,
        dimension_numbers=dimension_labels,
        preferred_element_type=jnp.float32,
    )


def silu_slope(pre_act):
    sigmoid_gate = jax.nn.sigmoid(pre_act)
    return sigmoid_gate * (1.0 + pre_act * (1.0 - sigmoid_gate))


def match_rows(pairing_row, branch, first_patch, patch_count):
    total_patches = pairing_row.shape[0]
    all_patches = jnp.arange(total_patches, dtype=jnp.int32)
    inverse = jnp.sum(
        jnp.where(pairing_row[:, None] == all_patches[None, :], all_patches[:, None], 0), axis=0
    )
    positions = first_patch + jnp.arange(patch_count, dtype=jnp.int32)
    return jnp.where(branch == 0, jnp.take(pairing_row, positions), jnp.take(inverse, positions))


def local(
    features_in,
    strided_weights,
    dilated_weights,
    tile_bias,
    cost_cotangent,
    footprint_pairing,
    valid_counts,
    tile_owner,
):
    scene_index = lax.axis_index("scene")
    tile_index = lax.axis_index("tile")
    branch = scene_index % 2
    pair_index = scene_index // 2
    features = features_in[0]
    own_cotangent = cost_cotangent[0]
    patches, channels, cells_in = (features.shape[0], features.shape[1], features.shape[2])
    cells_out = own_cotangent.shape[1]
    grid_side = math.isqrt(cells_in)
    half_side = grid_side // 2
    strided_kernel = lax.dynamic_index_in_dim(strided_weights, branch, 0, keepdims=False).reshape(
        channels, channels, 4, 4
    )
    dilated_kernel = lax.dynamic_index_in_dim(dilated_weights, branch, 0, keepdims=False).reshape(
        channels, channels, 3, 3
    )
    tile_id = lax.dynamic_index_in_dim(tile_owner, scene_index, 0, keepdims=False)
    bias_row = lax.dynamic_index_in_dim(tile_bias, tile_id, 0, keepdims=False)
    plain = ("NCHW", "OIHW", "NCHW")
    flipped = ("NCHW", "IOHW", "NCHW")
    kernel_side = ("CNHW", "IOHW", "CNHW")
    feature_grid = features.reshape(patches, channels, grid_side, grid_side)
    pre_act = (
        apply_convolution(
            feature_grid, strided_kernel, (2, 2), ((1, 1), (1, 1)), (1, 1), (1, 1), plain
        )
        + bias_row[None, :, None, None]
    )
    activation = jax.nn.silu(pre_act).astype(jnp.bfloat16)
    branch_grid = apply_convolution(
        activation, dilated_kernel, (1, 1), ((2, 2), (2, 2)), (1, 1), (2, 2), plain
    ).astype(jnp.bfloat16)
    branch_out = branch_grid.reshape(patches, channels, cells_out)
    pairing_row = lax.dynamic_index_in_dim(footprint_pairing, pair_index, 0, keepdims=False)
    first_patch = tile_index * patches
    swapped_out, swapped_cot = from_partner((branch_out, own_cotangent), "scene", 0)
    partner_out, partner_cot = (
        lax.all_gather(swapped_out, "tile", axis=0, tiled=True),
        lax.all_gather(swapped_cot, "tile", axis=0, tiled=True),
    )
    matched = match_rows(pairing_row, branch, first_patch, patches)
    chosen_out = jnp.take(partner_out, matched, axis=0)
    chosen_cot = jnp.take(partner_cot, matched, axis=0)
    pair_valid = lax.dynamic_index_in_dim(valid_counts, pair_index, 0, keepdims=False)
    live_count = jnp.clip(pair_valid - first_patch, 0, patches)
    live_mask = (jnp.arange(patches, dtype=jnp.int32) < live_count).astype(jnp.float32)
    signal = (own_cotangent.astype(jnp.float32) + chosen_cot.astype(jnp.float32)) * live_mask[
        :, None
    ]
    out_grad = (signal[:, None, :] * chosen_out.astype(jnp.float32)).astype(jnp.bfloat16)
    out_grid = out_grad.reshape(patches, channels, half_side, half_side)
    act_grad = apply_convolution(
        out_grid,
        dilated_kernel[:, :, ::-1, ::-1],
        (1, 1),
        ((2, 2), (2, 2)),
        (1, 1),
        (2, 2),
        flipped,
    )
    grad_dilated = apply_convolution(
        activation, out_grid, (2, 2), ((2, 2), (2, 2)), (1, 1), (1, 1), kernel_side
    )
    pre_grad = act_grad * silu_slope(pre_act)
    bias_grad = jnp.sum(pre_grad, axis=(0, 2, 3))
    pre_narrow = pre_grad.astype(jnp.bfloat16)
    grad_strided = apply_convolution(
        feature_grid, pre_narrow, (1, 1), ((1, 1), (1, 1)), (1, 1), (2, 2), kernel_side
    )
    feature_grad = apply_convolution(
        pre_narrow,
        strided_kernel[:, :, ::-1, ::-1],
        (1, 1),
        ((2, 2), (2, 2)),
        (2, 2),
        (1, 1),
        flipped,
    )
    feature_grads = feature_grad.astype(jnp.bfloat16).reshape(patches, channels, cells_in)
    grad_row = jnp.concatenate(
        [
            grad_strided.reshape(channels, 16 * channels),
            grad_dilated.reshape(channels, 9 * channels),
        ],
        axis=1,
    )
    scenes = lax.axis_size("scene")
    tile_devices = lax.axis_size("tile")
    weight_scale = 1.0 / math.sqrt(scenes * patches * tile_devices * cells_out)
    bias_scale = 1.0 / math.sqrt(patches * tile_devices * cells_out)
    branch_hit = jnp.arange(2, dtype=jnp.int32)[:, None, None] == branch
    weight_term = jnp.where(branch_hit, (grad_row * weight_scale)[None], jnp.float32(0.0)).reshape(
        2 * channels, 25 * channels
    )
    rows_each = 2 * channels // scenes
    summed = lax.psum(weight_term, ("scene", "tile"))
    grad_weights = lax.dynamic_slice_in_dim(summed, scene_index * rows_each, rows_each, 0)
    bias_rows = tile_bias.shape[0] // (scenes * tile_devices)
    scaled_bias = bias_grad * bias_scale
    owned_mask = tile_id == jnp.arange(
        lax.axis_size(("scene", "tile")) * bias_rows, dtype=jnp.int32
    )
    grad_bias = lax.psum_scatter(
        jnp.where(owned_mask[:, None], scaled_bias[None, :], jnp.float32(0.0)),
        ("scene", "tile"),
        scatter_dimension=0,
        tiled=True,
    )
    return (feature_grads[None], grad_weights, grad_bias)


def solution(mesh):
    return jax.shard_map(
        local,
        mesh=mesh,
        in_specs=(
            P("scene", "tile", None, None),
            P(),
            P(),
            P(),
            P("scene", "tile", None),
            P(),
            P(),
            P(),
        ),
        out_specs=(P("scene", "tile", None, None), P("scene", None), P(("scene", "tile"), None)),
        check_vma=False,
    )
```

profile of v0, /device:TPU:1, one launch (start us, length us, event | category | flops | bytes accessed | tf_op | source)
XLA Modules:
  0.0 380.0 jit_solution(3628517353644582072)
XLA Ops:
  7.2 3.3 collective-permute-start
  10.5 1.2 dynamic_slice.30
  13.1 0.9 constant_dynamic-slice_fusion.1
  14.2 0.8 copy.171
  15.2 1.0 copy.169
  16.2 2.3 reshape_squeeze.3
  18.5 2.9 copy.200
  21.4 3.4 fusion.59
  24.8 2.7 fusion.12
  27.5 6.3 %copy.167 = bf16[64,64,2,8,13]{0,3,2,4,1:T(8,128)(2,1)} copy(bf16[64,64,2,8,13]{1,0,4,3,2:T(8,128)(2,1)} %fusion.12) | data formatting | bytes 3407872 | tf_op jit(solution)/shard_map/conv_general_dilated | solution.py:22
  34.7 4.8 %fusion.27 = f32[32,16,5,64]{3,1,2,0:T(8,128)S(1)} fusion(bf16[64,64,4,4]{1,0,3,2:T(8,128)(2,1)S(1)} %copy-done.11, bf16[64,64,2,8,13]{0,3,2,4,1:T(8,128)(2,1)} %copy.167, f32[64]{0:T(128)S(1)} %dynamic-slice_reduce_fusion, pred[16,5]{0,1:T(8,128)(4,1)S(1)} %copy-done.17), kind=kOutput, calls=%fused_computation.39 | convolution fusion | flops 330629120 | bytes 2490704 | tf_op jit(solution)/shard_map/conv_general_dilated | solution.py:22
  40.6 1.7 convolution_convert_fusion.1
  42.5 1.0 copy.173
  43.7 1.2 iota_compare_fusion.9
  44.8 0.8 fusion.58
  45.6 3.6 fusion.57
  49.2 0.6 dynamic_slice.28
  50.7 0.6 gather_fusion.2
  51.4 0.6 gather_fusion.3
  52.0 4.2 %fusion.15 = (bf16[64,64,2,8,10]{1,0,4,3,2:T(8,128)(2,1)}, bf16[64,64,2,8,10]{1,0,4,3,2:T(8,128)(2,1)S(1)}) fusion(bf16[64,64,2,7,1]{1,0,4,3,2:T(8,128)(2,1)} %get-tuple-element.12, bf16[64,64,2,8,9]{1,0,4,3,2:T(8,128)(2,1)} %get-tuple-element.10, bf16[64,64,2,7,1]{1,0,4,3,2:T(8,128)(2,1)} %get-tuple-element.14, bf16[64,64,2,8,9]{1,0,4,3,2:T(8,128)(2,1)} %get-tuple-element.11), kind=kLoop, calls=%fused_computation.22 | loop fusion | flops 7864320 | bytes 5210112 | tf_op jit(solution)/shard_map/reshape;squeeze | solution.py:80
  56.3 0.7 slice.38
  57.0 0.9 copy-done.2
  57.9 2.3 fusion.17
  60.3 4.6 %copy.187 = bf16[64,64,2,8,10]{0,3,2,4,1:T(8,128)(2,1)} copy(bf16[64,64,2,8,10]{1,0,4,3,2:T(8,128)(2,1)} %copy-done.2) | data formatting | bytes 2621440 | tf_op jit(solution)/shard_map/reshape;squeeze | solution.py:80
  65.0 0.6 broadcast_in_dim.101
  65.8 2.9 copy.189
  68.8 4.8 %copy.185 = bf16[64,64,2,8,10]{0,3,2,4,1:T(8,128)(2,1)} copy(bf16[64,64,2,8,10]{1,0,4,3,2:T(8,128)(2,1)} %get-tuple-element.23) | data formatting | bytes 2621440 | tf_op jit(solution)/shard_map/reshape;squeeze | solution.py:80
  73.6 2.9 copy.188
  76.5 4.7 %all-gather = bf16[2,2,1024]{2,1,0:T(2,128)(2,1)S(1)} all-gather(bf16[1,2,1024]{2,1,0:T(2,128)(2,1)S(1)} %bitcast.88), channel_id=1, replica_groups=mesh['scene'=128,'tile'=2] {'tile'}, dimensions={0}, use_global_device_ids=true | all-gather | bytes 12288 | tf_op jit(solution)/shard_map/all_gather | solution.py:97
  81.3 0.6 gather_fusion
  82.0 1.2 copy.174
  83.2 8.5 %all_gather.7 = bf16[4,64,1024]{2,1,0:T(8,128)(2,1)S(1)} all-gather(bf16[2,64,1024]{2,1,0:T(8,128)(2,1)S(1)} %copy.174), channel_id=1, replica_groups=mesh['scene'=128,'tile'=2] {'tile'}, dimensions={0}, use_global_device_ids=true | all-gather | bytes 786432 | tf_op jit(solution)/shard_map/all_gather | solution.py:96
  91.7 0.6 gather_fusion.1
  93.5 3.1 fusion.49
  97.5 0.7 copy-done.9
  98.3 1.5 convert_select_fusion
  100.8 0.8 copy-done.7
  101.6 1.0 copy-done.4
  102.6 5.0 %fusion = f32[64,64,4,4,1]{0,1,3,4,2:T(8,128)S(1)} fusion(bf16[64,64,16,10,1]{0,2,4,3,1:T(8,128)(2,1)S(1)} %bitcast.81, bf16[64,64,16,10,1]{0,2,4,3,1:T(8,128)(2,1)S(1)} %bitcast.79, bf16[64,64,16,10,1]{0,2,4,3,1:T(8,128)(2,1)S(1)} %copy-done.5, bf16[64,64,16,10,1]{0,2,4,3,1:T(8,128)(2,1)S(1)} %bitcast.80, bf16[32,16,5,64]{3,1,2,0:T(8,128)(2,1)S(1)} %get-tuple-element.21), kind=kOutput, calls=%fused_computation.4 | convolution fusion | flops 351272960 | bytes 5832704 | tf_op jit(solution)/shard_map/conv_general_dilated | solution.py:22
  108.1 0.7 broadcast_select_fusion
  109.1 1.1 bitcast_select_fusion
  110.2 3.1 convolution_convert_fusion
  113.3 0.5 copy.182
  113.9 2.9 copy.183
  116.8 4.1 %broadcast_in_dim_reshape.3 = bf16[1,2,64,4096]{3,2,1,0:T(8,128)(2,1)} reshape(bf16[2,64,64,64]{3,2,1,0:T(8,128)(2,1)} %copy.183) | data formatting | bytes 2097152 | tf_op jit(solution)/shard_map/broadcast_in_dim;reshape | solution.py:167
  120.9 249.6 %all-reduce.4.cloned.1.call-done = (f32[128,1600]{1,0:T(8,128)}, f32[256,64]{1,0:T(8,128)}) async-done(((f32[128,1600]{1,0:T(8,128)}, f32[256,64]{1,0:T(8,128)}), (f32[128,1600]{1,0:T(8,128)}, f32[256,64]{1,0:T(8,128)})) %all-reduce.4.cloned.1.call-update) | async-done | bytes 884752 | tf_op jit(solution)/shard_map/psum | solution.py:154
  370.5 1.4 constant_dynamic-slice_fusion
  371.9 1.2 constant_dynamic-slice_fusion.3
  (89 shorter events, 6.9 us)
Async XLA Ops:
  7.2 7.9 %copy-start = (bf16[2,64,1024]{2,1,0:T(8,128)(2,1)S(1)}, bf16[2,64,1024]{2,1,0:T(8,128)(2,1)}, u32[]{:S(2)}) copy-start(bf16[2,64,1024]{2,1,0:T(8,128)(2,1)} %param.11) | copy-start | bytes 786436
  7.2 9.0 %copy-start.10 = (bf16[1,2,64,4096]{3,2,1,0:T(8,128)(2,1)S(1)}, bf16[1,2,64,4096]{3,2,1,0:T(8,128)(2,1)}, u32[]{:S(2)}) copy-start(bf16[1,2,64,4096]{3,2,1,0:T(8,128)(2,1)} %param.10) | copy-start | bytes 3145732
  7.2 363.3 %all-reduce.4.cloned.1.call-start = ((), (), s32[]{:S(2)}) async-start(), calls=%async_computation | async-start | bytes 1966080 | tf_op jit(solution)/shard_map/psum | solution.py:154
  7.2 69.3 %collective-permute-start = (bf16[2,1024]{1,0:T(2,128)(2,1)}, bf16[2,1024]{1,0:T(2,128)(2,1)S(1)}, u32[]{:S(2)}, u32[]{:S(2)}) collective-permute-start(bf16[2,1024]{1,0:T(2,128)(2,1)} %bitcast.87), channel_id=1, source_target_pairs={{0,2},{2,0},{4,6},{6,4},{8,10},{10,8},{12,14},{14,12},{16,18},{18,... | collective-permute-start | bytes 12296 | tf_op jit(solution)/shard_map/ppermute | solution.py:10
  27.5 7.0 %copy-start.15 = (f32[256,64]{0,1:T(8,128)S(1)}, f32[256,64]{0,1:T(8,128)}, u32[]{:S(2)}) copy-start(f32[256,64]{0,1:T(8,128)} %param.13) | copy-start | bytes 196612
  27.5 7.2 %copy-start.11 = (bf16[64,64,4,4]{1,0,3,2:T(8,128)(2,1)S(1)}, bf16[64,64,4,4]{1,0,3,2:T(8,128)(2,1)}, u32[]{:S(2)}) copy-start(bf16[64,64,4,4]{1,0,3,2:T(8,128)(2,1)} %copy.169) | copy-start | bytes 393220
  27.5 7.2 %copy-start.17 = (pred[16,5]{0,1:T(8,128)(4,1)S(1)}, pred[16,5]{0,1:T(8,128)(4,1)}, u32[]{:S(2)}) copy-start(pred[16,5]{0,1:T(8,128)(4,1)} %constant.131) | copy-start | bytes 244
  39.5 2.8 copy-start.8
  39.5 1.1 copy-start.13
  43.5 38.5 %collective-permute-start.1 = (bf16[2,64,1024]{1,2,0:T(8,128)(2,1)}, bf16[2,64,1024]{1,2,0:T(8,128)(2,1)}, u32[]{:S(2)}, u32[]{:S(2)}) collective-permute-start(bf16[2,64,1024]{1,2,0:T(8,128)(2,1)} %bitcast.12), channel_id=1, source_target_pairs={{0,2},{2,0},{4,6},{6,4},{8,10},{10,8},{12,14},{14,12},{16,18},{18,... | collective-permute-start | bytes 786440 | tf_op jit(solution)/shard_map/ppermute | solution.py:10
  45.6 3.6 copy-start.21
  45.6 4.8 %copy-start.18 = (s32[64,4]{0,1:T(4,128)S(1)}, s32[64,4]{0,1:T(4,128)}, u32[]{:S(2)}) copy-start(s32[64,4]{0,1:T(4,128)} %param.15) | copy-start | bytes 3076
  56.3 1.6 copy-start.2
  57.9 2.3 copy-start.16
  68.8 4.8 %copy-start.3 = (bf16[64,64,2,8,10]{1,0,4,3,2:T(8,128)(2,1)S(1)}, bf16[64,64,2,8,10]{1,0,4,3,2:T(8,128)(2,1)}, u32[]{:S(2)}) copy-start(bf16[64,64,2,8,10]{1,0,4,3,2:T(8,128)(2,1)} %fusion.17) | copy-start | bytes 3932164
  96.9 1.3 copy-start.9
  97.0 1.3 copy-start.14
  98.3 2.2 copy-start.5
  98.3 2.5 copy-start.6
  98.3 3.3 copy-start.7
  99.7 2.8 copy-start.4
  102.6 5.5 %copy-start.19 = (pred[256]{0:T(512)(128)(4,1)S(1)}, pred[256]{0:T(512)(128)(4,1)}, u32[]{:S(2)}) copy-start(pred[256]{0:T(512)(128)(4,1)} %iota_compare_fusion.9) | copy-start | bytes 772
  107.5 1.5 copy-start.20
  108.8 1.3 copy-start.12
  113.9 259.3 %copy-start.1 = (bf16[2,64,1024]{2,1,0:T(8,128)(2,1)S(1)}, bf16[2,64,1024]{2,1,0:T(8,128)(2,1)}, u32[]{:S(2)}) copy-start(bf16[2,64,1024]{2,1,0:T(8,128)(2,1)} %param.11) | copy-start | bytes 786436
Sparse Core Ops, SparseCore 0:
  110.3 260.1 all-reduce.3
where the time goes:
time: 382 us; the launch traced here: 380 us
  waiting for transfers between devices  250 us (65%)
  local copies, waits for them, and re-layouts  63 us (16%)
  matrix products  19.1 us (5%)
  between operations  17.1 us (4%)
  other arithmetic  14.5 us (4%)
  blocking collectives  13.2 us (3%)
    psum x1, waiting for transfers between devices, local(): summed = lax.psum(weight_term, ('scene', 'tile'))  250 us
    another operation x9, local copies, waits for them, and re-layouts, local(): feature_grid = features.reshape(patches, channels, grid_side, grid_side)  26 us
    conv_general_dilated x6, matrix products, apply_convolution(): lax.conv_general_dilated(left_operand, right_operand, window_strides, bor...  19.1 us
    unnamed x49, local copies, waits for them, and re-layouts  8.82 us
    all_gather x1, blocking collectives, local(): lax.all_gather(swapped_out, 'tile', axis=0, tiled=True)  8.5 us
  transfers between devices with their start and end apart: 3, of which 1 were waited for; matrix products, arithmetic and copies ran while one was open for 19% of the time, Pallas kernels for 0%

commit v1 on v0

v1 whole, which is shorter than its diff:
```python
import functools
import math

import jax
import jax.numpy as jnp
from jax import lax
from jax.experimental import pallas as pl
from jax.experimental.pallas import tpu as pltpu
from jax.sharding import PartitionSpec as P

F32 = jnp.float32
BF16 = jnp.bfloat16
MESH = pl.DeviceIdType.MESH

CH = 64
SIDE = 32
CELLS = SIDE * SIDE
GROUP = 512
GROUPS = 8
COLS = 1792
PATCHES = 2


def iota(shape, dim):
    return lax.broadcasted_iota(jnp.int32, shape, dim)


def dot(a, b):
    return lax.dot_general(a, b, (((1,), (0,)), ((), ())), preferred_element_type=F32)


def dot_nt(a, b):
    return lax.dot_general(a, b, (((1,), (1,)), ((), ())), preferred_element_type=F32)


def dot_tn(a, b):
    return lax.dot_general(a, b, (((0,), (0,)), ((), ())), preferred_element_type=F32)


def one_hot_columns(rows, target):
    cols = target.shape[1]
    hit = iota((rows, cols), 0) == target
    return jnp.where(hit, 1.0, 0.0).astype(BF16)


def column_taps():
    n = iota((1, 1024), 1)
    parity = n // 512
    tap = (n // 128) % 4
    row = (n % 128) // 32
    col = 2 * (n % 32) - 1 + tap
    target = (2 * row + parity) * 64 + col
    target = jnp.where((col >= 0) & (col < 64), target, -1)
    return one_hot_columns(GROUP, target)


def strided_order():
    n = iota((1, 1024), 1)
    return one_hot_columns(1024, (n % 64) * 16 + n // 64)


def dilated_order():
    n = iota((1, 768), 1)
    row, col, channel = n // 256, (n % 256) // 64, n % 64
    target = jnp.where(col < 3, channel * 9 + row * 3 + col, -1)
    return one_hot_columns(576, target)


def shift_rows(x, cells):
    lane = iota(x.shape, 1)
    moved = pltpu.roll(x, (-cells) % CELLS, 1)
    keep = lane < CELLS - cells if cells > 0 else lane >= -cells
    return jnp.where(keep, moved, 0.0)


def shift_cols(x, cells):
    col = iota(x.shape, 1) % SIDE
    moved = pltpu.roll(x, (-cells) % CELLS, 1)
    keep = col < SIDE - cells if cells > 0 else col >= -cells
    return jnp.where(keep, moved, 0.0)


def kernel(
    dims,
    feat,
    sw,
    dw,
    tb,
    cot,
    fp,
    vc,
    to,
    out_feat,
    out_gw,
    out_gb,
    xs,
    sel,
    perm_s,
    perm_d,
    wp,
    vp,
    taps,
    pre,
    act3,
    mine,
    theirs,
    their_cot,
    gr,
    pr,
    gw,
    acc,
    ysend,
    yrecv,
    zsend,
    zrecv,
    xsend,
    xrecv,
    bown,
    by,
    bz,
    bsend,
    brecv,
    stack,
    feat_out,
    in_sem,
    out_sem,
    ex_send,
    ex_recv,
    y_send,
    y_recv,
    z_send,
    z_recv,
    x_send,
    x_recv,
    bx_send,
    bx_recv,
):
    n_y, n_z = dims
    rows_own = CH // (2 * n_y * n_z)
    rows_z = 2 * rows_own
    rows_y = rows_z * n_z
    scene = lax.axis_index("scene")
    tile = lax.axis_index("tile")
    core = lax.rem(scene, 2)
    z = lax.rem(scene // 2, n_z)
    y = lax.rem(scene // (2 * n_z), n_y)
    x_lo = scene // (2 * n_z * n_y)
    pair = scene // 2

    def scene_of(xl, yy, zz, cc):
        return ((xl * n_y + yy) * n_z + zz) * 2 + cc

    def at_y(d):
        return lax.rem(y + d, n_y)

    def at_z(d):
        return lax.rem(z + d, n_z)

    def ring(k):
        return scene_of(k // 4, y, z, (k // 2) % 2), k % 2

    me_ring = x_lo * 4 + core * 2 + tile

    def other(k):
        return lax.rem(me_ring + k, 8)

    barrier = pltpu.get_barrier_semaphore()
    for d in range(1, n_y):
        pl.semaphore_signal(
            barrier, inc=1, device_id=(scene_of(x_lo, at_y(d), z, core), tile), device_id_type=MESH
        )
    for d in range(1, n_z):
        pl.semaphore_signal(
            barrier, inc=1, device_id=(scene_of(x_lo, y, at_z(d), core), tile), device_id_type=MESH
        )
    for k in range(1, 8):
        pl.semaphore_signal(barrier, inc=1, device_id=ring(other(k)), device_id_type=MESH)

    def load(p, h):
        return pltpu.make_async_copy(
            feat.at[0, p, :, pl.ds(h * GROUP, GROUP)], xs.at[p, h], in_sem.at[p, h]
        )

    for p in range(PATCHES):
        for h in range(GROUPS):
            load(p, h).start()

    sel[...] = column_taps()
    perm_s[...] = strided_order()
    perm_d[...] = dilated_order()
    w_all = dot(sw[core], perm_s[...]).astype(BF16)
    for slot, tap in enumerate((1, 3, 0, 2)):
        wp[slot * CH : (slot + 1) * CH, :] = w_all[:, tap * 256 : (tap + 1) * 256]
    v_all = dot(dw[core], perm_d[...]).astype(BF16)
    for tap in range(3):
        vp[tap * CH : (tap + 1) * CH, :] = v_all[:, tap * 256 : tap * 256 + 192]

    bias = jnp.sum(jnp.where(iota(tb.shape, 1) == to[scene], tb[...], 0.0), axis=1, keepdims=True)

    for p in range(PATCHES):
        for h in range(GROUPS):
            load(p, h).wait()
    for p in range(PATCHES):
        split = dot(xs[p].reshape(GROUPS * CH, GROUP), sel[...]).astype(BF16)
        for h in range(GROUPS):
            for n in range(8):
                taps[p, n * CH : (n + 1) * CH, h * 128 : (h + 1) * 128] = split[
                    h * CH : (h + 1) * CH, n * 128 : (n + 1) * 128
                ]

    def push(p, to_ring):
        return pltpu.make_async_remote_copy(
            src_ref=mine.at[p],
            dst_ref=theirs.at[tile * 2 + p],
            send_sem=ex_send.at[to_ring, p],
            recv_sem=ex_recv.at[tile, p],
            device_id=(scene_of(x_lo, y, z, 1 - core), tile if to_ring == 0 else 1 - tile),
            device_id_type=MESH,
        )

    def push_cot(to_ring):
        return pltpu.make_async_remote_copy(
            src_ref=cot.at[0],
            dst_ref=their_cot.at[tile],
            send_sem=ex_send.at[to_ring, 2],
            recv_sem=ex_recv.at[tile, 2],
            device_id=(scene_of(x_lo, y, z, 1 - core), tile if to_ring == 0 else 1 - tile),
            device_id_type=MESH,
        )

    def forward(p):
        even = dot(wp[0:128, :], taps[p, 0:256, :])
        odd = dot(wp[128:256, :], taps[p, 256:512, :])
        pre_act = (
            even[0:CH]
            + odd[CH:]
            + shift_rows(even[CH:], SIDE)
            + shift_rows(odd[0:CH], -SIDE)
            + bias
        )
        pre[p] = pre_act
        act = (pre_act * jax.nn.sigmoid(pre_act)).astype(BF16)
        wide = act.astype(F32)
        act3[p, 0:CH] = shift_cols(wide, -2).astype(BF16)
        act3[p, CH : 2 * CH] = act
        act3[p, 2 * CH :] = shift_cols(wide, 2).astype(BF16)
        rows = dot(vp[...], act3[p])
        out = (
            rows[CH : 2 * CH]
            + shift_rows(rows[0:CH], -2 * SIDE)
            + shift_rows(rows[2 * CH :], 2 * SIDE)
        )
        mine[p] = out.astype(BF16)

    forward(0)
    pl.semaphore_wait(barrier, (n_y - 1) + (n_z - 1) + 7)
    for to_ring in range(2):
        push_cot(to_ring).start()
        push(0, to_ring).start()
    forward(1)
    for to_ring in range(2):
        push(1, to_ring).start()

    def pairing(j):
        inverse = jnp.int32(0)
        for i in range(4):
            inverse = jnp.where(fp[i, pair] == j, i, inverse)
        return jnp.where(core == 0, fp[j, pair], inverse)

    live_count = vc[pair]

    for t in range(2):
        for p in range(3):
            if p < 2:
                pltpu.make_async_copy(mine.at[p], theirs.at[t * 2 + p], ex_recv.at[t, p]).wait()
            else:
                pltpu.make_async_copy(cot.at[0], their_cot.at[t], ex_recv.at[t, 2]).wait()

    bias_col = jnp.zeros((CH, 1), F32)
    for p in range(PATCHES):
        j = tile * PATCHES + p
        matched = pairing(j)
        partner_cot = jnp.zeros((1, CELLS), F32)
        for t in range(2):
            both = their_cot[t].astype(F32)
            for i in range(2):
                partner_cot = partner_cot + jnp.where(matched == t * 2 + i, both[i : i + 1], 0.0)
        own_cot = cot[0].astype(F32)[p : p + 1]
        live = jnp.where(j < live_count, 1.0, 0.0).astype(F32)
        signal = (own_cot + partner_cot) * live
        out_grad = (signal * theirs[matched].astype(F32)).astype(BF16)
        wide = out_grad.astype(F32)
        gr[0:CH] = shift_rows(wide, 2 * SIDE).astype(BF16)
        gr[CH : 2 * CH] = out_grad
        gr[2 * CH :] = shift_rows(wide, -2 * SIDE).astype(BF16)
        gdil = dot_nt(gr[...], act3[p])
        cols = dot_tn(vp[...], gr[...])
        act_grad = (
            cols[CH : 2 * CH] + shift_cols(cols[0:CH], 2) + shift_cols(cols[2 * CH :], -2)
        )
        v = pre[p]
        g = jax.nn.sigmoid(v)
        pre_grad = act_grad * (g * (1.0 + v * (1.0 - g)))
        bias_col = bias_col + jnp.sum(pre_grad, axis=1, keepdims=True)
        narrow = pre_grad.astype(BF16)
        wide = narrow.astype(F32)
        pr[p, 0:CH] = narrow
        pr[p, CH : 2 * CH] = shift_rows(wide, -SIDE).astype(BF16)
        pr[p, 2 * CH : 3 * CH] = shift_rows(wide, SIDE).astype(BF16)
        pr[p, 3 * CH :] = narrow
        geven = dot_nt(pr[p, 0:128], taps[p, 0:256])
        godd = dot_nt(pr[p, 128:256], taps[p, 256:512])
        for slot, tap in enumerate((1, 3, 0, 2)):
            part = (geven if slot < 2 else godd)[(slot % 2) * CH : (slot % 2 + 1) * CH]
            where = slice(tap * 256, (tap + 1) * 256)
            if p == 0:
                gw[:, where] = part
            else:
                gw[:, where] += part
        for tap in range(3):
            part = gdil[tap * CH : (tap + 1) * CH]
            where = slice(1024 + tap * 256, 1024 + tap * 256 + 192)
            if p == 0:
                gw[:, where] = part
                gw[:, 1024 + tap * 256 + 192 : 1024 + (tap + 1) * 256] = jnp.zeros((CH, 64), F32)
            else:
                gw[:, where] += part

    ysend[...] = gw[...].astype(BF16)
    wide_eye = iota((CH, 128), 0) == iota((CH, 128), 1)
    bown[...] = jnp.sum(
        jnp.where(wide_eye, jnp.broadcast_to(bias_col, (CH, 128)), 0.0), axis=0, keepdims=True
    )

    def y_copy(d):
        return pltpu.make_async_remote_copy(
            src_ref=ysend.at[pl.ds(pl.multiple_of(at_y(d) * rows_y, rows_y), rows_y), :],
            dst_ref=yrecv.at[y],
            send_sem=y_send.at[0, d],
            recv_sem=y_recv.at[0, y],
            device_id=(scene_of(x_lo, at_y(d), z, core), tile),
            device_id_type=MESH,
        )

    def by_copy(d):
        return pltpu.make_async_remote_copy(
            src_ref=bown,
            dst_ref=by.at[y],
            send_sem=y_send.at[1, d],
            recv_sem=y_recv.at[1, y],
            device_id=(scene_of(x_lo, at_y(d), z, core), tile),
            device_id_type=MESH,
        )

    for d in range(1, n_y):
        y_copy(d).start()
        by_copy(d).start()

    def store(p):
        return pltpu.make_async_copy(feat_out.at[p], out_feat.at[0, p], out_sem.at[p])

    def feature_grad(p):
        for half in range(2):
            part = dot_tn(
                wp[half * 128 : (half + 1) * 128, :], pr[p, half * 128 : (half + 1) * 128, :]
            ).astype(BF16)
            for h in range(GROUPS):
                for n in range(4):
                    stack[h * CH : (h + 1) * CH, (half * 4 + n) * 128 : (half * 4 + n + 1) * 128] = (
                        part[n * CH : (n + 1) * CH, h * 128 : (h + 1) * 128]
                    )
        whole = dot_nt(stack[...], sel[...]).astype(BF16)
        for h in range(GROUPS):
            feat_out[p, :, h * GROUP : (h + 1) * GROUP] = whole[h * CH : (h + 1) * CH]
        store(p).start()

    feature_grad(0)

    by[pl.ds(y, 1)] = bown[...][None]
    total = gw[pl.ds(pl.multiple_of(y * rows_y, rows_y), rows_y), :]
    for d in range(1, n_y):
        source = at_y(d)
        pltpu.make_async_copy(ysend.at[0:rows_y, :], yrecv.at[source], y_recv.at[0, source]).wait()
        total = total + yrecv[source].astype(F32)
    for d in range(1, n_y):
        source = at_y(d)
        pltpu.make_async_copy(bown, by.at[source], y_recv.at[1, source]).wait()
    for k in range(n_z):
        zsend[k] = total[k * rows_z : (k + 1) * rows_z]

    def z_copy(d):
        return pltpu.make_async_remote_copy(
            src_ref=zsend.at[at_z(d)],
            dst_ref=zrecv.at[z],
            send_sem=z_send.at[0, d],
            recv_sem=z_recv.at[0, z],
            device_id=(scene_of(x_lo, y, at_z(d), core), tile),
            device_id_type=MESH,
        )

    def bz_copy(d):
        return pltpu.make_async_remote_copy(
            src_ref=by,
            dst_ref=bz.at[z],
            send_sem=z_send.at[1, d],
            recv_sem=z_recv.at[1, z],
            device_id=(scene_of(x_lo, y, at_z(d), core), tile),
            device_id_type=MESH,
        )

    for d in range(1, n_z):
        z_copy(d).start()
        bz_copy(d).start()

    feature_grad(1)

    total = zsend[z]
    for d in range(1, n_z):
        source = at_z(d)
        pltpu.make_async_copy(zsend.at[0], zrecv.at[source], z_recv.at[0, source]).wait()
        total = total + zrecv[source]
    bz[pl.ds(z, 1)] = by[...][None]
    for d in range(1, n_z):
        source = at_z(d)
        pltpu.make_async_copy(by, bz.at[source], z_recv.at[1, source]).wait()
    for r in range(2):
        xsend[r] = total[r * rows_own : (r + 1) * rows_own]

    k8 = iota((8, 128), 0)
    tile_ids = scene_of(k8 // 4, y, z, (k8 // 2) % 2) * 2 + k8 % 2
    sums = jnp.zeros((8, 128), F32)
    for zz in range(n_z):
        for yy in range(n_y):
            owner = to[scene_of(x_lo, yy, zz, core)]
            sums = sums + jnp.where(tile_ids == owner, bz[zz, yy], 0.0)
    for k in range(8):
        bsend[k] = sums[k : k + 1]

    here = tile * 2 + x_lo

    def x_copy(r, t):
        return pltpu.make_async_remote_copy(
            src_ref=xsend.at[r],
            dst_ref=xrecv.at[here],
            send_sem=x_send.at[r, t],
            recv_sem=x_recv.at[here],
            device_id=(scene_of(core, y, z, r), t),
            device_id_type=MESH,
        )

    def is_me(r, t):
        return (x_lo == core) & (core == r) & (tile == t)

    def bx_copy(k):
        return pltpu.make_async_remote_copy(
            src_ref=bsend.at[other(k)],
            dst_ref=brecv.at[me_ring],
            send_sem=bx_send.at[k],
            recv_sem=bx_recv.at[me_ring],
            device_id=ring(other(k)),
            device_id_type=MESH,
        )

    for r in range(2):
        for t in range(2):

            @pl.when(jnp.logical_not(is_me(r, t)))
            def _():
                x_copy(r, t).start()

            @pl.when(is_me(r, t))
            def _():
                xrecv[pl.ds(here, 1)] = xsend[r][None]

    for k in range(1, 8):
        bx_copy(k).start()

    brecv[pl.ds(me_ring, 1)] = bsend[pl.ds(me_ring, 1)]
    for s in range(4):

        @pl.when(jnp.logical_not((core == x_lo) & (here == s)))
        def _():
            pltpu.make_async_copy(xsend.at[0], xrecv.at[s], x_recv.at[s]).wait()

    scale = 1.0 / math.sqrt(4 * n_y * n_z * PATCHES * 2 * CELLS)
    rows = (xrecv[0] + xrecv[1] + xrecv[2] + xrecv[3]) * scale
    sub = iota((16, COLS), 0)
    for r in range(rows_own):
        row = rows[r : r + 1]
        high = row.astype(BF16).astype(F32)
        rest = row - high
        middle = rest.astype(BF16).astype(F32)
        low = rest - middle
        parts = jnp.where(
            sub == 0, high, jnp.where(sub == 1, middle, jnp.where(sub == 2, low, 0.0))
        ).astype(BF16)
        strided = dot_nt(parts[:, 0:1024], perm_s[...])
        dilated = dot_nt(parts[:, 1024:], perm_d[...])
        out_gw[r : r + 1, 0:1024] = jnp.sum(strided, axis=0, keepdims=True)
        out_gw[r : r + 1, 1024:1600] = jnp.sum(dilated, axis=0, keepdims=True)

    for k in range(1, 8):
        source = other(k)
        pltpu.make_async_copy(bsend.at[0], brecv.at[source], bx_recv.at[source]).wait()
    bias_total = brecv[0]
    for k in range(1, 8):
        bias_total = bias_total + brecv[k]
    bias_scale = 1.0 / math.sqrt(2 * PATCHES * CELLS)
    out_gb[...] = bias_total[:, 0:CH] * bias_scale

    for p in range(PATCHES):
        store(p).wait()
    for to_ring in range(2):
        push_cot(to_ring).wait_send()
        for p in range(PATCHES):
            push(p, to_ring).wait_send()
    for d in range(1, n_y):
        y_copy(d).wait_send()
        by_copy(d).wait_send()
    for d in range(1, n_z):
        z_copy(d).wait_send()
        bz_copy(d).wait_send()
    for r in range(2):
        for t in range(2):

            @pl.when(jnp.logical_not(is_me(r, t)))
            def _():
                x_copy(r, t).wait_send()

    for k in range(1, 8):
        bx_copy(k).wait_send()


def grid_of(scenes):
    n_z = 8 if scenes == 128 else 1
    return scenes // (4 * n_z), n_z


def local(dims, features_in, sw, dw, tb, cot, fp, vc, to):
    n_y, n_z = dims
    rows_own = CH // (2 * n_y * n_z)
    rows_y = 2 * rows_own * n_z
    vmem = pl.BlockSpec(memory_space=pltpu.VMEM)
    smem = pl.BlockSpec(memory_space=pltpu.SMEM)
    anywhere = pl.BlockSpec(memory_space=pl.ANY)
    dma = pltpu.SemaphoreType.DMA
    V = pltpu.VMEM
    return pl.pallas_call(
        functools.partial(kernel, dims),
        out_shape=(
            jax.ShapeDtypeStruct(features_in.shape, BF16),
            jax.ShapeDtypeStruct((rows_own, 1600), F32),
            jax.ShapeDtypeStruct((1, CH), F32),
        ),
        in_specs=[anywhere, vmem, vmem, vmem, vmem, smem, smem, smem],
        out_specs=(anywhere, vmem, vmem),
        scratch_shapes=[
            V((PATCHES, GROUPS, CH, GROUP), BF16),
            V((GROUP, 1024), BF16),
            V((1024, 1024), BF16),
            V((576, 768), BF16),
            V((256, 256), BF16),
            V((192, 192), BF16),
            V((PATCHES, 512, CELLS), BF16),
            V((PATCHES, CH, CELLS), F32),
            V((PATCHES, 192, CELLS), BF16),
            V((PATCHES, CH, CELLS), BF16),
            V((4, CH, CELLS), BF16),
            V((2, 2, CELLS), BF16),
            V((192, CELLS), BF16),
            V((PATCHES, 256, CELLS), BF16),
            V((CH, COLS), F32),
            V((8, 128), F32),
            V((CH, COLS), BF16),
            V((n_y, rows_y, COLS), BF16),
            V((n_z, 2 * rows_own, COLS), F32),
            V((n_z, 2 * rows_own, COLS), F32),
            V((2, rows_own, COLS), F32),
            V((4, rows_own, COLS), F32),
            V((1, 128), F32),
            V((n_y, 1, 128), F32),
            V((n_z, n_y, 1, 128), F32),
            V((8, 1, 128), F32),
            V((8, 1, 128), F32),
            V((GROUPS * CH, 1024), BF16),
            V((PATCHES, CH, 4096), BF16),
            dma((PATCHES, GROUPS)),
            dma((PATCHES,)),
            dma((2, 3)),
            dma((2, 3)),
            dma((2, n_y)),
            dma((2, n_y)),
            dma((2, n_z)),
            dma((2, n_z)),
            dma((2, 2)),
            dma((4,)),
            dma((8,)),
            dma((8,)),
        ],
        compiler_params=pltpu.CompilerParams(
            collective_id=0, has_side_effects=True, vmem_limit_bytes=60 * 1024 * 1024
        ),
    )(features_in, sw, dw, tb.T, cot, fp.T, vc, to)


def solution(mesh):
    return jax.shard_map(
        functools.partial(local, grid_of(mesh.shape["scene"])),
        mesh=mesh,
        in_specs=(
            P("scene", "tile", None, None),
            P(),
            P(),
            P(),
            P("scene", "tile", None),
            P(),
            P(),
            P(),
        ),
        out_specs=(P("scene", "tile", None, None), P("scene", None), P(("scene", "tile"), None)),
        check_vma=False,
    )
```

time: 382 us -> 44.9 us (0.12)
  waiting for transfers between devices: 250 us -> 0 us
  local copies, waits for them, and re-layouts: 63 us -> 3.4 us
  Pallas kernels: 0 us -> 40.7 us
  matrix products: 19.1 us -> 0 us
  between operations: 17.1 us -> 0.65 us
  other arithmetic: 14.5 us -> 0 us
  blocking collectives: 13.2 us -> 0 us
    psum x1 -> x0, waiting for transfers between devices: 250 us -> none  [local(): summed = lax.psum(weight_term, ('scene', 'tile'))]
    pallas_call x0 -> x1, Pallas kernels: none -> 40.7 us  [local(): pl.pallas_call(functools.partial(kernel, dims), out_shape=(jax.ShapeDtype...]
    another operation x10 -> x0, local copies, waits for them, and re-layouts: 30.2 us -> none  [the longest x9 26 us: local(): feature_grid = features.reshape(patches, channels, grid_side, grid_side)]
    conv_general_dilated x6 -> x0, matrix products: 19.1 us -> none  [apply_convolution(): lax.conv_general_dilated(left_operand, right_operand, window_strides, bor...]
    all_gather x2 -> x0, blocking collectives: 13.2 us -> none  [the longest x1 8.5 us: local(): lax.all_gather(swapped_out, 'tile', axis=0, tiled=True)]
    conv_general_dilated x5 -> x0, local copies, waits for them, and re-layouts: 6.94 us -> none  [apply_convolution(): lax.conv_general_dilated(left_operand, right_operand, window_strides, bor...]
    another operation x2 -> x0, other arithmetic: 6.56 us -> none  [local(): feature_grid = features.reshape(patches, channels, grid_side, grid_side)]
    unnamed x49 -> x7, local copies, waits for them, and re-layouts: 8.82 us -> 3.4 us
  transfers between devices with their start and end apart: 3 -> 0, of which waited for: 1 -> 0; matrix products, arithmetic and copies ran while one was open for 19% -> 0% of each run, Pallas kernels for 0% -> 0%
where the time goes in v1:
time: 44.9 us; the launch traced here: 44.7 us
  Pallas kernels  40.7 us (91%)
  local copies, waits for them, and re-layouts  3.4 us (8%)
  between operations  0.65 us (1%)
    pallas_call x1, Pallas kernels, local(): pl.pallas_call(functools.partial(kernel, dims), out_shape=(jax.ShapeDtype...  40.7 us
    unnamed x7, local copies, waits for them, and re-layouts  3.4 us

profile of v1, /device:TPU:1, one launch (start us, length us, event | category | flops | bytes accessed | tf_op | source)
XLA Modules:
  0.0 44.7 jit_solution(2304857619270823309)
XLA Ops:
  0.6 40.7 %shard_map.103 = (bf16[1,2,64,4096]{3,2,1,0:T(8,128)(2,1)}, f32[1,1600]{1,0:T(1,128)}, f32[1,64]{1,0:T(1,128)}) custom-call(bf16[1,2,64,4096]{3,2,1,0:T(8,128)(2,1)} %feat.1, bf16[2,64,1024]{2,1,0:T(8,128)(2,1)} %sw.1, bf16[2,64,576]{2,1,0:T(8,128)(2,1)} %dw.1, f32[64,256]{1,0:T(8,128)} %bitcast.2, bf16[1,2,1024]{2,1,0:T(2,128)(2,1)} %cot.1, ...), custom_call_target="tpu_custom_call" | custom-call | tf_op jit(solution)/shard_map/pallas_call | solution.py:548
  41.3 0.0 copy-start
  41.3 2.3 %copy.14 = bf16[1,2,64,4096]{3,2,1,0:T(8,128)(2,1)} copy(bf16[1,2,64,4096]{3,2,1,0:T(8,128)(2,1)} %get-tuple-element.6) | data formatting | bytes 2097152
  43.6 0.0 copy-done
  43.6 0.0 copy-start.1
  43.6 0.6 %copy.15 = f32[1,1600]{1,0:T(1,128)} copy(f32[1,1600]{1,0:T(1,128)S(1)} %copy-done) | data formatting | bytes 12800
  44.2 0.0 copy-done.1
  44.2 0.5 %copy.16 = f32[1,64]{1,0:T(1,128)} copy(f32[1,64]{1,0:T(1,128)S(1)} %copy-done.1) | data formatting | bytes 512
Async XLA Ops:
  41.3 2.3 %copy-start = (f32[1,1600]{1,0:T(1,128)S(1)}, f32[1,1600]{1,0:T(1,128)}, u32[]{:S(2)}) copy-start(f32[1,1600]{1,0:T(1,128)} %get-tuple-element.7) | copy-start | bytes 19204
  43.6 0.6 %copy-start.1 = (f32[1,64]{1,0:T(1,128)S(1)}, f32[1,64]{1,0:T(1,128)}, u32[]{:S(2)}) copy-start(f32[1,64]{1,0:T(1,128)} %get-tuple-element.8) | copy-start | bytes 772

commit v2 on v1

v2 whole, which is shorter than its diff:
```python
import functools
import math

import jax
import jax.numpy as jnp
from jax import lax
from jax.experimental import pallas as pl
from jax.experimental.pallas import tpu as pltpu
from jax.sharding import PartitionSpec as P

F32 = jnp.float32
BF16 = jnp.bfloat16
MESH = pl.DeviceIdType.MESH

CH = 64
SIDE = 32
CELLS = SIDE * SIDE
GROUP = 512
GROUPS = 8
COLS = (768, 1024)
PATCHES = 2


def iota(shape, dim):
    return lax.broadcasted_iota(jnp.int32, shape, dim)


def dot(a, b):
    return lax.dot_general(a, b, (((1,), (0,)), ((), ())), preferred_element_type=F32)


def dot_nt(a, b):
    return lax.dot_general(a, b, (((1,), (1,)), ((), ())), preferred_element_type=F32)


def dot_tn(a, b):
    return lax.dot_general(a, b, (((0,), (0,)), ((), ())), preferred_element_type=F32)


def one_hot_columns(rows, target):
    cols = target.shape[1]
    hit = iota((rows, cols), 0) == target
    return jnp.where(hit, 1.0, 0.0).astype(BF16)


def column_taps():
    n = iota((1, 1024), 1)
    parity = n // 512
    tap = (n // 128) % 4
    row = (n % 128) // 32
    col = 2 * (n % 32) - 1 + tap
    target = (2 * row + parity) * 64 + col
    target = jnp.where((col >= 0) & (col < 64), target, -1)
    return one_hot_columns(GROUP, target)


def strided_order():
    n = iota((1, 1024), 1)
    return one_hot_columns(1024, (n % 64) * 16 + n // 64)


def dilated_order():
    n = iota((1, 768), 1)
    row, col, channel = n // 256, (n % 256) // 64, n % 64
    target = jnp.where(col < 3, channel * 9 + row * 3 + col, -1)
    return one_hot_columns(576, target)


def shift_rows(x, cells):
    lane = iota(x.shape, 1)
    moved = pltpu.roll(x, (-cells) % CELLS, 1)
    keep = lane < CELLS - cells if cells > 0 else lane >= -cells
    return jnp.where(keep, moved, 0.0)


def shift_cols(x, cells):
    col = iota(x.shape, 1) % SIDE
    moved = pltpu.roll(x, (-cells) % CELLS, 1)
    keep = col < SIDE - cells if cells > 0 else col >= -cells
    return jnp.where(keep, moved, 0.0)


def kernel(
    dims,
    feat,
    sw_in,
    dw_in,
    tb_in,
    cot_in,
    fp_in,
    vc_in,
    to_in,
    out_feat,
    out_a,
    out_b,
    out_bias,
    sw,
    dw,
    tb,
    cot,
    fp,
    vc,
    to,
    xs,
    sel,
    perm_s,
    perm_d,
    wp,
    vp,
    taps,
    pre,
    act3,
    mine,
    theirs,
    their_cot,
    gr,
    pr,
    gw_a,
    gw_b,
    ysend_a,
    ysend_b,
    yrecv_a,
    yrecv_b,
    zsend_a,
    zsend_b,
    zrecv_a,
    zrecv_b,
    xsend_a,
    xsend_b,
    xrecv_a,
    xrecv_b,
    bown,
    by,
    bz,
    bsend,
    brecv,
    stack,
    feat_out,
    w_sem,
    in_sem,
    out_sem,
    ex_send,
    ex_recv,
    y_send,
    y_recv,
    z_send,
    z_recv,
    x_send,
    x_recv,
    bx_send,
    bx_recv,
):
    n_y, n_z = dims
    rows_own = CH // (2 * n_y * n_z)
    rows_z = 2 * rows_own
    rows_y = rows_z * n_z
    gw = (gw_a, gw_b)
    ysend = (ysend_a, ysend_b)
    yrecv = (yrecv_a, yrecv_b)
    zsend = (zsend_a, zsend_b)
    zrecv = (zrecv_a, zrecv_b)
    xsend = (xsend_a, xsend_b)
    xrecv = (xrecv_a, xrecv_b)
    scene = lax.axis_index("scene")
    tile = lax.axis_index("tile")
    core = lax.rem(scene, 2)
    z = lax.rem(scene // 2, n_z)
    y = lax.rem(scene // (2 * n_z), n_y)
    x_lo = scene // (2 * n_z * n_y)
    pair = scene // 2

    def scene_of(xl, yy, zz, cc):
        return ((xl * n_y + yy) * n_z + zz) * 2 + cc

    def at_y(d):
        return lax.rem(y + d, n_y)

    def at_z(d):
        return lax.rem(z + d, n_z)

    def ring(k):
        return scene_of(k // 4, y, z, (k // 2) % 2), k % 2

    me_ring = x_lo * 4 + core * 2 + tile

    def other(k):
        return lax.rem(me_ring + k, 8)

    def load(p, h):
        return pltpu.make_async_copy(
            feat.at[0, p, :, pl.ds(h * GROUP, GROUP)], xs.at[p, h], in_sem.at[p, h]
        )

    def load_small(i):
        source, target = (
            (sw_in.at[core], sw),
            (dw_in.at[core], dw),
            (tb_in, tb),
            (cot_in.at[0], cot),
            (fp_in, fp),
            (vc_in, vc),
            (to_in, to),
        )[i]
        return pltpu.make_async_copy(source, target, w_sem.at[i])

    load_small(0).start()
    load_small(1).start()
    for h in range(GROUPS):
        load(0, h).start()
    for i in range(2, 7):
        load_small(i).start()
    for h in range(GROUPS):
        load(1, h).start()

    barrier = pltpu.get_barrier_semaphore()
    for d in range(1, n_y):
        pl.semaphore_signal(
            barrier, inc=1, device_id=(scene_of(x_lo, at_y(d), z, core), tile), device_id_type=MESH
        )
    for d in range(1, n_z):
        pl.semaphore_signal(
            barrier, inc=1, device_id=(scene_of(x_lo, y, at_z(d), core), tile), device_id_type=MESH
        )
    for k in range(1, 8):
        pl.semaphore_signal(barrier, inc=1, device_id=ring(other(k)), device_id_type=MESH)

    sel[...] = column_taps()
    perm_s[...] = strided_order()
    perm_d[...] = dilated_order()
    load_small(0).wait()
    w_all = dot(sw[...], perm_s[...]).astype(BF16)
    for slot, tap in enumerate((1, 3, 0, 2)):
        wp[slot * CH : (slot + 1) * CH, :] = w_all[:, tap * 256 : (tap + 1) * 256]
    load_small(1).wait()
    v_all = dot(dw[...], perm_d[...]).astype(BF16)
    for tap in range(3):
        vp[tap * CH : (tap + 1) * CH, :] = v_all[:, tap * 256 : tap * 256 + 192]
    for i in range(2, 7):
        load_small(i).wait()
    bias = jnp.sum(jnp.where(iota(tb.shape, 1) == to[scene], tb[...], 0.0), axis=1, keepdims=True)

    def split(p):
        for h in range(GROUPS):
            load(p, h).wait()
        parts = dot(xs[p].reshape(GROUPS * CH, GROUP), sel[...]).astype(BF16)
        for h in range(GROUPS):
            for n in range(8):
                taps[p, n * CH : (n + 1) * CH, h * 128 : (h + 1) * 128] = parts[
                    h * CH : (h + 1) * CH, n * 128 : (n + 1) * 128
                ]

    def partner(to_ring):
        return scene_of(x_lo, y, z, 1 - core), tile if to_ring == 0 else 1 - tile

    def push(p, to_ring):
        return pltpu.make_async_remote_copy(
            src_ref=mine.at[p],
            dst_ref=theirs.at[tile * 2 + p],
            send_sem=ex_send.at[to_ring, p],
            recv_sem=ex_recv.at[tile, p],
            device_id=partner(to_ring),
            device_id_type=MESH,
        )

    def push_cot(to_ring):
        return pltpu.make_async_remote_copy(
            src_ref=cot,
            dst_ref=their_cot.at[tile],
            send_sem=ex_send.at[to_ring, 2],
            recv_sem=ex_recv.at[tile, 2],
            device_id=partner(to_ring),
            device_id_type=MESH,
        )

    def forward(p):
        even = dot(wp[0:128, :], taps[p, 0:256, :])
        odd = dot(wp[128:256, :], taps[p, 256:512, :])
        pre_act = (
            even[0:CH]
            + odd[CH:]
            + shift_rows(even[CH:], SIDE)
            + shift_rows(odd[0:CH], -SIDE)
            + bias
        )
        pre[p] = pre_act
        act = (pre_act * jax.nn.sigmoid(pre_act)).astype(BF16)
        wide = act.astype(F32)
        act3[p, 0:CH] = shift_cols(wide, -2).astype(BF16)
        act3[p, CH : 2 * CH] = act
        act3[p, 2 * CH :] = shift_cols(wide, 2).astype(BF16)
        rows = dot(vp[...], act3[p])
        out = (
            rows[CH : 2 * CH]
            + shift_rows(rows[0:CH], -2 * SIDE)
            + shift_rows(rows[2 * CH :], 2 * SIDE)
        )
        mine[p] = out.astype(BF16)

    for p in range(PATCHES):
        split(p)
        forward(p)
        if p == 0:
            pl.semaphore_wait(barrier, (n_y - 1) + (n_z - 1) + 7)
        for to_ring in (1, 0):
            push(p, to_ring).start()
            if p == 0:
                push_cot(to_ring).start()

    for p in range(PATCHES):
        v = pre[p]
        g = jax.nn.sigmoid(v)
        pre[p] = g * (1.0 + v * (1.0 - g))

    def pairing(j):
        inverse = jnp.int32(0)
        for i in range(4):
            inverse = jnp.where(fp[i, pair] == j, i, inverse)
        return jnp.where(core == 0, fp[j, pair], inverse)

    live_count = vc[pair]

    for t in range(2):
        for p in range(3):
            if p < 2:
                pltpu.make_async_copy(mine.at[p], theirs.at[t * 2 + p], ex_recv.at[t, p]).wait()
            else:
                pltpu.make_async_copy(cot, their_cot.at[t], ex_recv.at[t, 2]).wait()

    def y_copy(c, d):
        return pltpu.make_async_remote_copy(
            src_ref=ysend[c].at[pl.ds(pl.multiple_of(at_y(d) * rows_y, rows_y), rows_y), :],
            dst_ref=yrecv[c].at[y],
            send_sem=y_send.at[c, d],
            recv_sem=y_recv.at[c, y],
            device_id=(scene_of(x_lo, at_y(d), z, core), tile),
            device_id_type=MESH,
        )

    def by_copy(d):
        return pltpu.make_async_remote_copy(
            src_ref=bown,
            dst_ref=by.at[y],
            send_sem=y_send.at[2, d],
            recv_sem=y_recv.at[2, y],
            device_id=(scene_of(x_lo, at_y(d), z, core), tile),
            device_id_type=MESH,
        )

    def z_copy(c, d):
        return pltpu.make_async_remote_copy(
            src_ref=zsend[c].at[at_z(d)],
            dst_ref=zrecv[c].at[z],
            send_sem=z_send.at[c, d],
            recv_sem=z_recv.at[c, z],
            device_id=(scene_of(x_lo, y, at_z(d), core), tile),
            device_id_type=MESH,
        )

    def bz_copy(d):
        return pltpu.make_async_remote_copy(
            src_ref=by,
            dst_ref=bz.at[z],
            send_sem=z_send.at[2, d],
            recv_sem=z_recv.at[2, z],
            device_id=(scene_of(x_lo, y, at_z(d), core), tile),
            device_id_type=MESH,
        )

    here = tile * 2 + x_lo

    def x_copy(c, r, t):
        return pltpu.make_async_remote_copy(
            src_ref=xsend[c].at[r],
            dst_ref=xrecv[c].at[here],
            send_sem=x_send.at[c, r, t],
            recv_sem=x_recv.at[c, here],
            device_id=(scene_of(core, y, z, r), t),
            device_id_type=MESH,
        )

    def is_me(r, t):
        return (x_lo == core) & (core == r) & (tile == t)

    def bx_copy(k):
        return pltpu.make_async_remote_copy(
            src_ref=bsend.at[other(k)],
            dst_ref=brecv.at[me_ring],
            send_sem=bx_send.at[k],
            recv_sem=bx_recv.at[me_ring],
            device_id=ring(other(k)),
            device_id_type=MESH,
        )

    def start_y(c):
        ysend[c][...] = gw[c][...].astype(BF16)
        for d in range(n_y - 1, 0, -1):
            y_copy(c, d).start()

    def y_to_z(c):
        total = gw[c][pl.ds(pl.multiple_of(y * rows_y, rows_y), rows_y), :]
        for d in range(1, n_y):
            source = at_y(d)
            pltpu.make_async_copy(
                ysend[c].at[0:rows_y, :], yrecv[c].at[source], y_recv.at[c, source]
            ).wait()
            total = total + yrecv[c][source].astype(F32)
        for k in range(n_z):
            zsend[c][k] = total[k * rows_z : (k + 1) * rows_z].astype(BF16)
        for d in range(1, n_z):
            z_copy(c, d).start()

    def z_to_x(c):
        total = zsend[c][z].astype(F32)
        for d in range(1, n_z):
            source = at_z(d)
            pltpu.make_async_copy(zsend[c].at[0], zrecv[c].at[source], z_recv.at[c, source]).wait()
            total = total + zrecv[c][source].astype(F32)
        for r in range(2):
            xsend[c][r] = total[r * rows_own : (r + 1) * rows_own]
        for r in range(2):
            for t in range(2):

                @pl.when(jnp.logical_not(is_me(r, t)))
                def _():
                    x_copy(c, r, t).start()

                @pl.when(is_me(r, t))
                def _():
                    xrecv[c][pl.ds(here, 1)] = xsend[c][r][None]

    def x_done(c, out):
        for s in range(4):

            @pl.when(jnp.logical_not((core == x_lo) & (here == s)))
            def _():
                pltpu.make_async_copy(xsend[c].at[0], xrecv[c].at[s], x_recv.at[c, s]).wait()

        out[...] = xrecv[c][0] + xrecv[c][1] + xrecv[c][2] + xrecv[c][3]

    for p in range(PATCHES):
        j = tile * PATCHES + p
        matched = pairing(j)
        partner_cot = jnp.zeros((1, CELLS), F32)
        for t in range(2):
            both = their_cot[t].astype(F32)
            for i in range(2):
                partner_cot = partner_cot + jnp.where(matched == t * 2 + i, both[i : i + 1], 0.0)
        own_cot = cot[...].astype(F32)[p : p + 1]
        live = jnp.where(j < live_count, 1.0, 0.0).astype(F32)
        signal = (own_cot + partner_cot) * live
        out_grad = (signal * theirs[matched].astype(F32)).astype(BF16)
        wide = out_grad.astype(F32)
        gr[p, 0:CH] = shift_rows(wide, 2 * SIDE).astype(BF16)
        gr[p, CH : 2 * CH] = out_grad
        gr[p, 2 * CH :] = shift_rows(wide, -2 * SIDE).astype(BF16)
        gdil = dot_nt(gr[p], act3[p])
        for tap in range(3):
            part = gdil[tap * CH : (tap + 1) * CH]
            where = slice(tap * 256, tap * 256 + 192)
            if p == 0:
                gw_a[:, where] = part
                gw_a[:, tap * 256 + 192 : (tap + 1) * 256] = jnp.zeros((CH, 64), F32)
            else:
                gw_a[:, where] += part
    start_y(0)

    bias_col = jnp.zeros((CH, 1), F32)
    for p in range(PATCHES):
        cols = dot_tn(vp[...], gr[p])
        act_grad = (
            cols[CH : 2 * CH] + shift_cols(cols[0:CH], 2) + shift_cols(cols[2 * CH :], -2)
        )
        pre_grad = act_grad * pre[p]
        bias_col = bias_col + jnp.sum(pre_grad, axis=1, keepdims=True)
        narrow = pre_grad.astype(BF16)
        wide = narrow.astype(F32)
        pr[p, 0:CH] = narrow
        pr[p, CH : 2 * CH] = shift_rows(wide, -SIDE).astype(BF16)
        pr[p, 2 * CH : 3 * CH] = shift_rows(wide, SIDE).astype(BF16)
        pr[p, 3 * CH :] = narrow
        geven = dot_nt(pr[p, 0:128], taps[p, 0:256])
        godd = dot_nt(pr[p, 128:256], taps[p, 256:512])
        for slot, tap in enumerate((1, 3, 0, 2)):
            part = (geven if slot < 2 else godd)[(slot % 2) * CH : (slot % 2 + 1) * CH]
            where = slice(tap * 256, (tap + 1) * 256)
            if p == 0:
                gw_b[:, where] = part
            else:
                gw_b[:, where] += part
    start_y(1)

    wide_eye = iota((CH, 128), 0) == iota((CH, 128), 1)
    bown[...] = jnp.sum(
        jnp.where(wide_eye, jnp.broadcast_to(bias_col, (CH, 128)), 0.0), axis=0, keepdims=True
    )
    for d in range(1, n_y):
        by_copy(d).start()
    by[pl.ds(y, 1)] = bown[...][None]

    def store(p):
        return pltpu.make_async_copy(feat_out.at[p], out_feat.at[0, p], out_sem.at[p])

    def feature_grad(p):
        for half in range(2):
            part = dot_tn(
                wp[half * 128 : (half + 1) * 128, :], pr[p, half * 128 : (half + 1) * 128, :]
            ).astype(BF16)
            for h in range(GROUPS):
                for n in range(4):
                    stack[h * CH : (h + 1) * CH, (half * 4 + n) * 128 : (half * 4 + n + 1) * 128] = (
                        part[n * CH : (n + 1) * CH, h * 128 : (h + 1) * 128]
                    )
        whole = dot_nt(stack[...], sel[...]).astype(BF16)
        for h in range(GROUPS):
            feat_out[p, :, h * GROUP : (h + 1) * GROUP] = whole[h * CH : (h + 1) * CH]
        store(p).start()

    feature_grad(0)
    y_to_z(0)
    feature_grad(1)
    y_to_z(1)
    for d in range(1, n_y):
        source = at_y(d)
        pltpu.make_async_copy(bown, by.at[source], y_recv.at[2, source]).wait()
    for d in range(1, n_z):
        bz_copy(d).start()
    z_to_x(0)
    z_to_x(1)

    bz[pl.ds(z, 1)] = by[...][None]
    for d in range(1, n_z):
        source = at_z(d)
        pltpu.make_async_copy(by, bz.at[source], z_recv.at[2, source]).wait()
    k8 = iota((8, 128), 0)
    tile_ids = scene_of(k8 // 4, y, z, (k8 // 2) % 2) * 2 + k8 % 2
    sums = jnp.zeros((8, 128), F32)
    for zz in range(n_z):
        for yy in range(n_y):
            owner = to[scene_of(x_lo, yy, zz, core)]
            sums = sums + jnp.where(tile_ids == owner, bz[zz, yy], 0.0)
    for k in range(8):
        bsend[k] = sums[k : k + 1]
    for k in range(1, 8):
        bx_copy(k).start()
    brecv[pl.ds(me_ring, 1)] = bsend[pl.ds(me_ring, 1)]

    x_done(0, out_a)
    x_done(1, out_b)
    for k in range(1, 8):
        source = other(k)
        pltpu.make_async_copy(bsend.at[0], brecv.at[source], bx_recv.at[source]).wait()
    bias_total = brecv[0]
    for k in range(1, 8):
        bias_total = bias_total + brecv[k]
    out_bias[...] = bias_total

    for p in range(PATCHES):
        store(p).wait()
    for to_ring in range(2):
        push_cot(to_ring).wait_send()
        for p in range(PATCHES):
            push(p, to_ring).wait_send()
    for d in range(1, n_y):
        for c in range(2):
            y_copy(c, d).wait_send()
        by_copy(d).wait_send()
    for d in range(1, n_z):
        for c in range(2):
            z_copy(c, d).wait_send()
        bz_copy(d).wait_send()
    for c in range(2):
        for r in range(2):
            for t in range(2):

                @pl.when(jnp.logical_not(is_me(r, t)))
                def _():
                    x_copy(c, r, t).wait_send()

    for k in range(1, 8):
        bx_copy(k).wait_send()


def pick(row, vregs, out_cols, taps, slot_of):
    split = jnp.concatenate([row[:, q * 128 : (q + 1) * 128] for q in range(vregs)], axis=0)
    if vregs < 8:
        split = jnp.concatenate([split, jnp.zeros((8 - vregs, 128), F32)], axis=0)
    high = split.astype(BF16).astype(F32)
    rest = split - high
    middle = rest.astype(BF16).astype(F32)
    low = rest - middle
    parts = jnp.concatenate([high, middle, low], axis=0).astype(BF16)
    lane = iota((1, out_cols), 1)
    slot = slot_of(lane % taps)
    sub = iota((8, out_cols), 0)
    total = jnp.zeros((8, out_cols), F32)
    for half in range(2):
        spread = dot(parts, one_hot_columns(128, half * 64 + lane // taps))
        hit = sub * 2 + half == slot
        total = total + jnp.where(hit, spread[0:8] + spread[8:16] + spread[16:24], 0.0)
    return jnp.sum(total, axis=0, keepdims=True)


def finish(dims, feat_in, row_a, row_b, bias, out_feat, out_gw, out_gb, sem):
    n_y, n_z = dims
    rows_own = CH // (2 * n_y * n_z)
    copy = pltpu.make_async_copy(feat_in, out_feat, sem)
    copy.start()
    scale = 1.0 / math.sqrt(4 * n_y * n_z * PATCHES * 2 * CELLS)
    for r in range(rows_own):
        out_gw[r : r + 1, 0:1024] = (
            pick(row_b[r : r + 1], 8, 1024, 16, lambda t: t) * scale
        )
        out_gw[r : r + 1, 1024:1600] = (
            pick(row_a[r : r + 1], 6, 576, 9, lambda t: t // 3 * 4 + t % 3) * scale
        )
    out_gb[...] = bias[:, 0:CH] * (1.0 / math.sqrt(2 * PATCHES * CELLS))
    copy.wait()


def grid_of(scenes):
    n_z = 8 if scenes == 128 else 1
    return scenes // (4 * n_z), n_z


def local(dims, features_in, sw, dw, tb, cot, fp, vc, to):
    n_y, n_z = dims
    rows_own = CH // (2 * n_y * n_z)
    rows_y = 2 * rows_own * n_z
    vmem = pl.BlockSpec(memory_space=pltpu.VMEM)
    hbm = pl.BlockSpec(memory_space=pltpu.HBM)
    anywhere = pl.BlockSpec(memory_space=pl.ANY)
    dma = pltpu.SemaphoreType.DMA
    V = pltpu.VMEM
    pairs = [
        (lambda c: V((CH, c), F32)),
        (lambda c: V((CH, c), BF16)),
        (lambda c: V((n_y, rows_y, c), BF16)),
        (lambda c: V((n_z, 2 * rows_own, c), BF16)),
        (lambda c: V((n_z, 2 * rows_own, c), BF16)),
        (lambda c: V((2, rows_own, c), F32)),
        (lambda c: V((4, rows_own, c), F32)),
    ]
    feat, row_a, row_b, bias = pl.pallas_call(
        functools.partial(kernel, dims),
        out_shape=(
            jax.ShapeDtypeStruct(features_in.shape, BF16),
            jax.ShapeDtypeStruct((rows_own, COLS[0]), F32),
            jax.ShapeDtypeStruct((rows_own, COLS[1]), F32),
            jax.ShapeDtypeStruct((1, 128), F32),
        ),
        in_specs=[hbm] * 8,
        out_specs=(anywhere, vmem, vmem, vmem),
        scratch_shapes=[
            V((CH, 1024), BF16),
            V((CH, 576), BF16),
            V(tb.shape[::-1], F32),
            V((PATCHES, CELLS), BF16),
            pltpu.SMEM(fp.shape[::-1], jnp.int32),
            pltpu.SMEM(vc.shape, jnp.int32),
            pltpu.SMEM(to.shape, jnp.int32),
            V((PATCHES, GROUPS, CH, GROUP), BF16),
            V((GROUP, 1024), BF16),
            V((1024, 1024), BF16),
            V((576, 768), BF16),
            V((256, 256), BF16),
            V((192, 192), BF16),
            V((PATCHES, 512, CELLS), BF16),
            V((PATCHES, CH, CELLS), F32),
            V((PATCHES, 192, CELLS), BF16),
            V((PATCHES, CH, CELLS), BF16),
            V((4, CH, CELLS), BF16),
            V((2, 2, CELLS), BF16),
            V((PATCHES, 192, CELLS), BF16),
            V((PATCHES, 256, CELLS), BF16),
            *[make(c) for make in pairs for c in COLS],
            V((1, 128), F32),
            V((n_y, 1, 128), F32),
            V((n_z, n_y, 1, 128), F32),
            V((8, 1, 128), F32),
            V((8, 1, 128), F32),
            V((GROUPS * CH, 1024), BF16),
            V((PATCHES, CH, 4096), BF16),
            dma((7,)),
            dma((PATCHES, GROUPS)),
            dma((PATCHES,)),
            dma((2, 3)),
            dma((2, 3)),
            dma((3, n_y)),
            dma((3, n_y)),
            dma((3, n_z)),
            dma((3, n_z)),
            dma((2, 2, 2)),
            dma((2, 4)),
            dma((8,)),
            dma((8,)),
        ],
        compiler_params=pltpu.CompilerParams(
            collective_id=0, has_side_effects=True, vmem_limit_bytes=48 * 1024 * 1024
        ),
    )(
        *(
            pltpu.with_memory_space_constraint(a, pltpu.HBM)
            for a in (features_in, sw, dw, tb.T, cot, fp.T, vc, to)
        )
    )
    return pl.pallas_call(
        functools.partial(finish, dims),
        out_shape=(
            jax.ShapeDtypeStruct(features_in.shape, BF16),
            jax.ShapeDtypeStruct((rows_own, 1600), F32),
            jax.ShapeDtypeStruct((1, CH), F32),
        ),
        in_specs=[anywhere, vmem, vmem, vmem],
        out_specs=(hbm, vmem, vmem),
        scratch_shapes=[dma],
        compiler_params=pltpu.CompilerParams(vmem_limit_bytes=16 * 1024 * 1024),
    )(feat, row_a, row_b, bias)


def solution(mesh):
    return jax.shard_map(
        functools.partial(local, grid_of(mesh.shape["scene"])),
        mesh=mesh,
        in_specs=(
            P("scene", "tile", None, None),
            P(),
            P(),
            P(),
            P("scene", "tile", None),
            P(),
            P(),
            P(),
        ),
        out_specs=(P("scene", "tile", None, None), P("scene", None), P(("scene", "tile"), None)),
        check_vma=False,
    )
```

time: 44.9 us -> 37.1 us (0.83)
  Pallas kernels: 40.7 us -> 36.4 us
  local copies, waits for them, and re-layouts: 3.4 us -> 0 us
    pallas_call x1, Pallas kernels: 40.7 us -> 34.8 us  [local(): pl.pallas_call(functools.partial(kernel, dims), out_shape=(jax.ShapeDtype...]
    unnamed x7 -> x0, local copies, waits for them, and re-layouts: 3.4 us -> none
    pallas_call x0 -> x1, Pallas kernels: none -> 1.58 us  [local(): pl.pallas_call(functools.partial(finish, dims), out_shape=(jax.ShapeDtype...]
where the time goes in v2:
time: 37.1 us; the launch traced here: 37 us
  Pallas kernels  36.4 us (98%)
  between operations  0.64 us (2%)
    pallas_call x1, Pallas kernels, local(): pl.pallas_call(functools.partial(kernel, dims), out_shape=(jax.ShapeDtype...  34.8 us
    pallas_call x1, Pallas kernels, local(): pl.pallas_call(functools.partial(finish, dims), out_shape=(jax.ShapeDtype...  1.58 us

profile of v2, /device:TPU:1, one launch (start us, length us, event | category | flops | bytes accessed | tf_op | source)
XLA Modules:
  0.0 37.0 jit_solution(12780613080606651930)
XLA Ops:
  0.6 34.8 %shard_map.103 = (bf16[1,2,64,4096]{3,2,1,0:T(8,128)(2,1)S(1)}, f32[1,768]{1,0:T(1,128)S(1)}, f32[1,1024]{1,0:T(1,128)S(1)}, f32[1,128]{1,0:T(1,128)S(1)}) custom-call(bf16[1,2,64,4096]{3,2,1,0:T(8,128)(2,1)} %feat.1, bf16[2,64,1024]{2,1,0:T(8,128)(2,1)} %sw_in.1, bf16[2,64,576]{2,1,0:T(8,128)(2,1)} %dw_in.1, f32[64,256]{1,0:T(8,128)} %bitcast.2, ...), custom_call_target="tpu_custom_call" | custom-call | tf_op jit(solution)/shard_map/pallas_call | solution.py:643
  35.4 1.6 %shard_map.104 = (bf16[1,2,64,4096]{3,2,1,0:T(8,128)(2,1)}, f32[1,1600]{1,0:T(1,128)}, f32[1,64]{1,0:T(1,128)}) custom-call(bf16[1,2,64,4096]{3,2,1,0:T(8,128)(2,1)S(1)} %get-tuple-element.7.feat_in, f32[1,768]{1,0:T(1,128)S(1)} %get-tuple-element.8.row_a, f32[1,1024]{1,0:T(1,128)S(1)} %get-tuple-element.9.row_b, f32[1,128]{1,0:T(1,128)S(1)} %get-tuple-element.10.bias), custom_call_target="tpu_custom_call" | custom-call | tf_op jit(solution)/shard_map/pallas_call | solution.py:706

commit v3 on v2

--- a/solution.py
+++ b/solution.py
@@ -33,37 +33,27 @@
     return lax.dot_general(a, b, (((1,), (1,)), ((), ())), preferred_element_type=F32)
 
 
-def dot_tn(a, b):
-    return lax.dot_general(a, b, (((0,), (0,)), ((), ())), preferred_element_type=F32)
-
-
 def one_hot_columns(rows, target):
     cols = target.shape[1]
     hit = iota((rows, cols), 0) == target
     return jnp.where(hit, 1.0, 0.0).astype(BF16)
 
 
-def column_taps():
-    n = iota((1, 1024), 1)
-    parity = n // 512
-    tap = (n // 128) % 4
-    row = (n % 128) // 32
-    col = 2 * (n % 32) - 1 + tap
-    target = (2 * row + parity) * 64 + col
-    target = jnp.where((col >= 0) & (col < 64), target, -1)
-    return one_hot_columns(GROUP, target)
-
-
-def strided_order():
-    n = iota((1, 1024), 1)
-    return one_hot_columns(1024, (n % 64) * 16 + n // 64)
-
-
-def dilated_order():
-    n = iota((1, 768), 1)
-    row, col, channel = n // 256, (n % 256) // 64, n % 64
-    target = jnp.where(col < 3, channel * 9 + row * 3 + col, -1)
-    return one_hot_columns(576, target)
+def column_taps(sel):
+    lane = iota((CH, 128), 1)
+    column = iota((CH, 128), 0)
+    zero = jnp.zeros((CH, 512), BF16)
+    for tap in range(4):
+        ones = jnp.where(column == 2 * (lane % SIDE) - 1 + tap, 1.0, 0.0)
+        for row in range(4):
+            block = jnp.where(lane // SIDE == row, ones, 0.0).astype(BF16)
+            for parity in range(2):
+                top = (2 * row + parity) * CH
+                left = parity * 512 + tap * 128
+                sel[top : top + CH, left : left + 128] = block
+    for row in range(8):
+        left = 512 - row % 2 * 512
+        sel[row * CH : (row + 1) * CH, left : left + 512] = zero
 
 
 def shift_rows(x, cells):
@@ -103,10 +93,12 @@
     to,
     xs,
     sel,
-    perm_s,
-    perm_d,
+    turned_s,
+    turned_d,
     wp,
+    wt,
     vp,
+    vt,
     taps,
     pre,
     act3,
@@ -224,17 +216,27 @@
     for k in range(1, 8):
         pl.semaphore_signal(barrier, inc=1, device_id=ring(other(k)), device_id_type=MESH)
 
-    sel[...] = column_taps()
-    perm_s[...] = strided_order()
-    perm_d[...] = dilated_order()
+    column_taps(sel)
+
     load_small(0).wait()
-    w_all = dot(sw[...], perm_s[...]).astype(BF16)
-    for slot, tap in enumerate((1, 3, 0, 2)):
-        wp[slot * CH : (slot + 1) * CH, :] = w_all[:, tap * 256 : (tap + 1) * 256]
+    turned_s[...] = sw[...].T.astype(F32)
+    for half, rows in enumerate(((1, 3), (0, 2))):
+        for col in range(4):
+            block = jnp.concatenate(
+                [turned_s[pl.ds(row * 4 + col, CH, stride=16), :] for row in rows], axis=1
+            )
+            block = block.astype(BF16)
+            wt[half, col * CH : (col + 1) * CH, :] = block
+            wp[half * 128 : (half + 1) * 128, col * CH : (col + 1) * CH] = block.T
     load_small(1).wait()
-    v_all = dot(dw[...], perm_d[...]).astype(BF16)
-    for tap in range(3):
-        vp[tap * CH : (tap + 1) * CH, :] = v_all[:, tap * 256 : tap * 256 + 192]
+    turned_d[...] = dw[...].T.astype(F32)
+    for col in range(3):
+        block = jnp.concatenate(
+            [turned_d[pl.ds(row * 3 + col, CH, stride=9), :] for row in range(3)], axis=1
+        )
+        block = block.astype(BF16)
+        vt[col * CH : (col + 1) * CH, :] = block
+        vp[:, col * CH : (col + 1) * CH] = block.T
     for i in range(2, 7):
         load_small(i).wait()
     bias = jnp.sum(jnp.where(iota(tb.shape, 1) == to[scene], tb[...], 0.0), axis=1, keepdims=True)
@@ -466,7 +468,7 @@
 
     bias_col = jnp.zeros((CH, 1), F32)
     for p in range(PATCHES):
-        cols = dot_tn(vp[...], gr[p])
+        cols = dot(vt[...], gr[p])
         act_grad = (
             cols[CH : 2 * CH] + shift_cols(cols[0:CH], 2) + shift_cols(cols[2 * CH :], -2)
         )
@@ -502,9 +504,7 @@
 
     def feature_grad(p):
         for half in range(2):
-            part = dot_tn(
-                wp[half * 128 : (half + 1) * 128, :], pr[p, half * 128 : (half + 1) * 128, :]
-            ).astype(BF16)
+            part = dot(wt[half], pr[p, half * 128 : (half + 1) * 128, :]).astype(BF16)
             for h in range(GROUPS):
                 for n in range(4):
                     stack[h * CH : (h + 1) * CH, (half * 4 + n) * 128 : (half * 4 + n + 1) * 128] = (
@@ -660,9 +660,11 @@
             pltpu.SMEM(to.shape, jnp.int32),
             V((PATCHES, GROUPS, CH, GROUP), BF16),
             V((GROUP, 1024), BF16),
-            V((1024, 1024), BF16),
-            V((576, 768), BF16),
+            V((1024, CH), F32),
+            V((576, CH), F32),
             V((256, 256), BF16),
+            V((2, 256, 128), BF16),
+            V((192, 192), BF16),
             V((192, 192), BF16),
             V((PATCHES, 512, CELLS), BF16),
             V((PATCHES, CH, CELLS), F32),

time: 37.1 us -> 37.1 us (level)
  no operation moved by 1% of the time
where the time goes in v3:
time: 37.1 us; the launch traced here: 37 us
  Pallas kernels  36.3 us (98%)
  between operations  0.64 us (2%)
    pallas_call x1, Pallas kernels, local(): pl.pallas_call(functools.partial(kernel, dims), out_shape=(jax.ShapeDtype...  34.8 us
    pallas_call x1, Pallas kernels, local(): pl.pallas_call(functools.partial(finish, dims), out_shape=(jax.ShapeDtype...  1.58 us

profile of v3, /device:TPU:1, one launch (start us, length us, event | category | flops | bytes accessed | tf_op | source)
XLA Modules:
  0.0 37.0 jit_solution(4090525680368052089)
XLA Ops:
  0.6 34.8 %shard_map.103 = (bf16[1,2,64,4096]{3,2,1,0:T(8,128)(2,1)S(1)}, f32[1,768]{1,0:T(1,128)S(1)}, f32[1,1024]{1,0:T(1,128)S(1)}, f32[1,128]{1,0:T(1,128)S(1)}) custom-call(bf16[1,2,64,4096]{3,2,1,0:T(8,128)(2,1)} %feat.1, bf16[2,64,1024]{2,1,0:T(8,128)(2,1)} %sw_in.1, bf16[2,64,576]{2,1,0:T(8,128)(2,1)} %dw_in.1, f32[64,256]{1,0:T(8,128)} %bitcast.2, ...), custom_call_target="tpu_custom_call" | custom-call | tf_op jit(solution)/shard_map/pallas_call | solution.py:643
  35.4 1.6 %shard_map.104 = (bf16[1,2,64,4096]{3,2,1,0:T(8,128)(2,1)}, f32[1,1600]{1,0:T(1,128)}, f32[1,64]{1,0:T(1,128)}) custom-call(bf16[1,2,64,4096]{3,2,1,0:T(8,128)(2,1)S(1)} %get-tuple-element.7.feat_in, f32[1,768]{1,0:T(1,128)S(1)} %get-tuple-element.8.row_a, f32[1,1024]{1,0:T(1,128)S(1)} %get-tuple-element.9.row_b, f32[1,128]{1,0:T(1,128)S(1)} %get-tuple-element.10.bias), custom_call_target="tpu_custom_call" | custom-call | tf_op jit(solution)/shard_map/pallas_call | solution.py:708
